TPU v7x, 32 devices: a whole 2x2x4 slice. The times are simulated.
32 devices in a mesh: dp: 16 (over z, x, core), tensor: 2 (over y).
Axes of the slice: x: 2, y: 2, z: 4, core: 2. Of those that a mesh axis runs over, the one named last changes fastest.
Arguments:
- inputs: float32 [16, 256, 768], P('dp'), may hold values from -6 to 6
- condition: float32 [16, 768], P('dp'), may hold values from -2.5 to 2.5
- cotangent: float32 [16, 256, 768], P('dp'), may hold values from -6 to 6
- w_qkv: float32 [2, 768, 3, 768], P(None, None, None, 'tensor'), may hold values from -0.21875 to 0.21875
- b_qv: float32 [2, 2, 768], P(None, None, 'tensor'), may hold values from -1.25 to 1.25
- w_out: float32 [2, 768, 768], P(None, 'tensor'), may hold values from -0.875 to 0.875
- b_out: float32 [2, 768], replicated, may hold values from -3 to 3
- w_up: float32 [2, 768, 3072], P(None, None, 'tensor'), may hold values from -0.21875 to 0.21875
- b_up: float32 [2, 3072], P(None, 'tensor'), may hold values from -3 to 3
- w_down: float32 [2, 3072, 768], P(None, 'tensor'), may hold values from -0.109375 to 0.109375
- b_down: float32 [2, 768], replicated, may hold values from -3 to 3
- w_mod: float32 [2, 768, 4608], P(None, None, 'tensor'), may hold values from -0.21875 to 0.21875
- b_mod: float32 [2, 4608], P(None, 'tensor'), may hold values from -0.75 to 0.75
Outputs:
- outputs: float32 [16, 256, 768], P('dp')
- grad_inputs: float32 [16, 256, 768], P('dp')
- grad_condition: float32 [16, 768], P('dp')
- grad_w_qkv: float32 [2, 768, 3, 768], P(None, 'dp', None, 'tensor')
- grad_b_qv: float32 [2, 2, 768], P(None, None, 'tensor')
- grad_w_out: float32 [2, 768, 768], P(None, 'tensor', 'dp')
- grad_b_out: float32 [2, 768], replicated
- grad_w_up: float32 [2, 768, 3072], P(None, 'dp', 'tensor')
- grad_b_up: float32 [2, 3072], P(None, 'tensor')
- grad_w_down: float32 [2, 3072, 768], P(None, 'tensor', 'dp')
- grad_b_down: float32 [2, 768], replicated
- grad_w_mod: float32 [2, 768, 4608], P(None, 'dp', 'tensor')
- grad_b_mod: float32 [2, 4608], P(None, 'tensor')
All inputs are finite; a program needn't handle non-finite values.
Results may differ from a plain program's by a relative error of at most 0.0003.
Values sent between devices are 32-bit elements; how exact they have to be, the bound alone decides.
A program may use at most 256 MiB of HBM per device.

v0:
```python
import jax
import jax.numpy as jnp
from jax import lax
from jax.sharding import PartitionSpec as P

HEAD_DIM = 64
high = lax.Precision.HIGH
eps_norm = 1e-06


def layer_norm(values):
    row_mean = jnp.mean(values, axis=-1, keepdims=True)
    centred = values - row_mean
    row_var = jnp.mean(centred * centred, axis=-1, keepdims=True)
    return centred * lax.rsqrt(row_var + eps_norm)


def gelu_tanh(values):
    return jax.nn.gelu(values, approximate=True)


def silu_slope(values):
    sigma = jax.nn.sigmoid(values)
    return sigma * (1.0 + values * (1.0 - sigma))


def pair_sum(value):
    if lax.axis_size("tensor") == 2:
        return value + lax.ppermute(value, "tensor", [(0, 1), (1, 0)])
    return lax.psum(value, "tensor")


def pair_gather(value, axis):
    if lax.axis_size("tensor") == 2:
        other = lax.ppermute(value, "tensor", [(0, 1), (1, 0)])
        first = lax.axis_index("tensor") == 0
        low = jnp.where(first, value, other)
        top = jnp.where(first, other, value)
        return jnp.concatenate([low, top], axis=axis)
    return lax.all_gather(value, "tensor", axis=axis, tiled=True)


def vec_mat(vec, mat):
    if vec.shape[0] == 1:
        return jnp.sum(vec[0][:, None] * mat, axis=0)[None]
    return jnp.einsum("bk,km->bm", vec, mat, precision=high)


def vec_mat_t(vec, mat):
    if vec.shape[0] == 1:
        return jnp.sum(vec[0][None, :] * mat, axis=1)[None]
    return jnp.einsum("bm,km->bk", vec, mat, precision=high)


def scattered_grad(left, right):
    tokens = left.shape[0] * left.shape[1]
    rows = left.shape[2]
    cols = right.shape[2]
    left_t = left.reshape(tokens, rows).T
    right = right.reshape(tokens, cols)
    count = lax.axis_size("dp")
    if count & count - 1 or count < 2:
        whole = jnp.dot(left_t, right, precision=high)
        return lax.psum_scatter(whole, "dp", scatter_dimension=0, tiled=True)
    block = rows // count
    index = lax.axis_index("dp")
    bit = index % 2
    blocks = left_t.reshape(count // 2, 2, block, tokens)

    def product(which):
        chosen = lax.dynamic_index_in_dim(blocks, which, 1, keepdims=False)
        return jnp.dot(chosen.reshape(rows // 2, tokens), right, precision=high)

    pairs = [(device, device ^ 1) for device in range(count)]
    arrived = lax.ppermute(product(1 - bit), "dp", pairs)
    total = product(bit) + arrived
    step = 2
    groups = count // 2
    while groups > 1:
        bit = index // step % 2
        parts = total.reshape(groups // 2, 2, block, cols)
        away = lax.dynamic_index_in_dim(parts, 1 - bit, 1, keepdims=False)
        kept = lax.dynamic_index_in_dim(parts, bit, 1, keepdims=False)
        pairs = [(device, device ^ step) for device in range(count)]
        total = kept + lax.ppermute(away, "dp", pairs)
        groups //= 2
        step *= 2
    return total.reshape(block, cols)


def on_device(
    inputs,
    condition,
    cotangent,
    w_qkv,
    b_qv,
    w_out,
    b_out,
    w_up,
    b_up,
    w_down,
    b_down,
    w_mod,
    b_mod,
):
    layers = w_qkv.shape[0]
    batch, seq_len, width = inputs.shape
    local_width = w_qkv.shape[3]
    heads_local = local_width // HEAD_DIM
    mod_cols = w_mod.shape[2]
    score_scale = HEAD_DIM ** (-0.5)
    activated = jax.nn.silu(condition)
    mod_local = (
        jnp.stack([vec_mat(activated, w_mod[index]) for index in range(layers)], axis=0)
        + b_mod[:, None, :]
    )
    mod_whole = pair_gather(mod_local, 2).reshape(layers, batch, 6, width)
    activated_all = lax.all_gather(activated, "dp", axis=0, tiled=True)
    kept = []
    hidden = inputs
    for layer_index in range(layers):
        modulation = mod_whole[layer_index]
        shift_a, scale_a, gate_a = (modulation[:, 0], modulation[:, 1], modulation[:, 2])
        shift_b, scale_b, gate_b = (modulation[:, 3], modulation[:, 4], modulation[:, 5])
        modul_a = layer_norm(hidden) * (1.0 + scale_a[:, None, :]) + shift_a[:, None, :]
        projected = jnp.einsum("bsd,dcm->bscm", modul_a, w_qkv[layer_index], precision=high)
        queries = (projected[:, :, 0] + b_qv[layer_index, 0]).reshape(
            batch, seq_len, heads_local, HEAD_DIM
        )
        keys = projected[:, :, 1].reshape(batch, seq_len, heads_local, HEAD_DIM)
        values = (projected[:, :, 2] + b_qv[layer_index, 1]).reshape(
            batch, seq_len, heads_local, HEAD_DIM
        )
        scores = jnp.einsum("bqhe,bkhe->bhqk", queries, keys, precision=high) * score_scale
        log_norm = jax.nn.logsumexp(scores, axis=-1, keepdims=True)
        probs = jnp.exp(scores - log_norm)
        attended = jnp.einsum("bhqk,bkhe->bqhe", probs, values, precision=high).reshape(
            batch, seq_len, local_width
        )
        partial_a = jnp.einsum("bsh,hd->bsd", attended, w_out[layer_index], precision=high)
        attn_branch = pair_sum(partial_a) + b_out[layer_index]
        middle = hidden + gate_a[:, None, :] * attn_branch
        modul_b = layer_norm(middle) * (1.0 + scale_b[:, None, :]) + shift_b[:, None, :]
        pre_act = (
            jnp.einsum("bsd,df->bsf", modul_b, w_up[layer_index], precision=high)
            + b_up[layer_index]
        )
        activ = gelu_tanh(pre_act)
        partial_b = jnp.einsum("bsf,fd->bsd", activ, w_down[layer_index], precision=high)
        mlp_branch = pair_sum(partial_b) + b_down[layer_index]
        result = middle + gate_b[:, None, :] * mlp_branch
        kept.append(
            (
                hidden,
                modul_a,
                queries,
                keys,
                values,
                probs,
                attended,
                attn_branch,
                middle,
                modul_b,
                pre_act,
                activ,
                mlp_branch,
            )
        )
        hidden = result
    grad_hidden = cotangent
    silu_grad_part = jnp.zeros((batch, width), jnp.float32)
    matrix_grads = [None] * layers
    pieces = [None] * layers
    for layer_index in reversed(range(layers)):
        (
            layer_in,
            modul_a,
            queries,
            keys,
            values,
            probs,
            attended,
            attn_branch,
            middle,
            modul_b,
            pre_act,
            activ,
            mlp_branch,
        ) = kept[layer_index]
        modulation = mod_whole[layer_index]
        scale_a, gate_a = (modulation[:, 1], modulation[:, 2])
        scale_b, gate_b = (modulation[:, 4], modulation[:, 5])
        d_branch_b = grad_hidden * gate_b[:, None, :]
        d_gate_b = jnp.sum(grad_hidden * mlp_branch, axis=1)
        g_b_down = jnp.sum(d_branch_b, axis=(0, 1))
        g_w_down = scattered_grad(d_branch_b, activ)
        d_activ = jnp.einsum("bsd,fd->bsf", d_branch_b, w_down[layer_index], precision=high)
        d_pre = jax.vjp(gelu_tanh, pre_act)[1](d_activ)[0]
        g_b_up = jnp.sum(d_pre, axis=(0, 1))
        g_w_up = scattered_grad(modul_b, d_pre)
        d_modul_b = pair_sum(jnp.einsum("bsf,df->bsd", d_pre, w_up[layer_index], precision=high))
        normed_b, norm_back_b = jax.vjp(layer_norm, middle)
        d_scale_b = jnp.sum(d_modul_b * normed_b, axis=1)
        d_shift_b = jnp.sum(d_modul_b, axis=1)
        d_middle = grad_hidden + norm_back_b(d_modul_b * (1.0 + scale_b[:, None, :]))[0]
        d_branch_a = d_middle * gate_a[:, None, :]
        d_gate_a = jnp.sum(d_middle * attn_branch, axis=1)
        g_b_out = jnp.sum(d_branch_a, axis=(0, 1))
        g_w_out = scattered_grad(d_branch_a, attended)
        d_attended = jnp.einsum(
            "bsd,hd->bsh", d_branch_a, w_out[layer_index], precision=high
        ).reshape(batch, seq_len, heads_local, HEAD_DIM)
        d_values = jnp.einsum("bhqk,bqhe->bkhe", probs, d_attended, precision=high)
        d_probs = jnp.einsum("bqhe,bkhe->bhqk", d_attended, values, precision=high)
        attended_heads = attended.reshape(batch, seq_len, heads_local, HEAD_DIM)
        row_dot = jnp.transpose(jnp.sum(d_attended * attended_heads, axis=-1), (0, 2, 1))[..., None]
        d_scores = probs * (d_probs - row_dot) * score_scale
        d_queries = jnp.einsum("bhqk,bkhe->bqhe", d_scores, keys, precision=high)
        d_keys = jnp.einsum("bhqk,bqhe->bkhe", d_scores, queries, precision=high)
        d_proj = jnp.stack([d_queries, d_keys, d_values], axis=2).reshape(
            batch, seq_len, 3, local_width
        )
        d_flat = d_proj.reshape(batch, seq_len, 3 * local_width)
        g_b_qv = jnp.sum(d_flat, axis=(0, 1))
        g_w_qkv = scattered_grad(modul_a, d_flat)
        d_modul_a = pair_sum(
            jnp.einsum("bscm,dcm->bsd", d_proj, w_qkv[layer_index], precision=high)
        )
        normed_a, norm_back_a = jax.vjp(layer_norm, layer_in)
        d_scale_a = jnp.sum(d_modul_a * normed_a, axis=1)
        d_shift_a = jnp.sum(d_modul_a, axis=1)
        grad_hidden = d_middle + norm_back_a(d_modul_a * (1.0 + scale_a[:, None, :]))[0]
        d_mod = jnp.stack(
            [d_shift_a, d_scale_a, d_gate_a, d_shift_b, d_scale_b, d_gate_b], axis=1
        ).reshape(batch, 6 * width)
        own_cols = lax.dynamic_slice_in_dim(d_mod, lax.axis_index("tensor") * mod_cols, mod_cols, 1)
        silu_grad_part = silu_grad_part + vec_mat_t(own_cols, w_mod[layer_index])
        matrix_grads[layer_index] = (g_w_qkv, g_w_out, g_w_up, g_w_down)
        pieces[layer_index] = (own_cols, (g_b_qv, g_b_out, g_b_up, g_b_down))
    block = width // lax.axis_size("dp")
    activated_rows = lax.dynamic_slice_in_dim(activated_all, lax.axis_index("dp") * block, block, 1)
    mod_grads = [None] * layers
    bias_grads = [None] * layers
    for layer_index in reversed(range(layers)):
        own_cols, biases = pieces[layer_index]
        line = jnp.concatenate(biases)[None]
        line = jnp.concatenate([line, jnp.zeros((batch - 1, line.shape[1]), line.dtype)], axis=0)
        gathered = lax.all_gather(
            jnp.concatenate([own_cols, line], axis=1), "dp", axis=0, tiled=True
        )
        mod_grads[layer_index] = jnp.einsum(
            "bd,bm->dm", activated_rows, gathered[:, :mod_cols], precision=high
        )
        sums = jnp.sum(gathered, axis=0)
        found = [sums[:mod_cols]]
        start = mod_cols
        for piece in biases:
            found.append(sums[start : start + piece.shape[0]])
            start += piece.shape[0]
        bias_grads[layer_index] = found
    order = range(layers)
    grad_w_qkv = jnp.stack([matrix_grads[index][0] for index in order], axis=0)
    grad_w_out = jnp.stack([matrix_grads[index][1].T for index in order], axis=0)
    grad_w_up = jnp.stack([matrix_grads[index][2] for index in order], axis=0)
    grad_w_down = jnp.stack([matrix_grads[index][3].T for index in order], axis=0)
    grad_b_mod, grad_b_qkv, grad_b_out, grad_b_up, grad_b_down = [
        jnp.stack([bias_grads[index][member] for index in order], axis=0) for member in range(5)
    ]
    grad_b_qv = grad_b_qkv.reshape(layers, 3, local_width)[:, ::2]
    grad_condition = pair_sum(silu_grad_part) * silu_slope(condition)
    return (
        hidden,
        grad_hidden,
        grad_condition,
        grad_w_qkv.reshape(layers, block, 3, local_width),
        grad_b_qv,
        grad_w_out,
        grad_b_out,
        grad_w_up,
        grad_b_up,
        grad_w_down,
        grad_b_down,
        jnp.stack(mod_grads, axis=0),
        grad_b_mod,
    )


def solution(mesh):
    in_specs = (
        P("dp", None, None),
        P("dp", None),
        P("dp", None, None),
        P(None, None, None, "tensor"),
        P(None, None, "tensor"),
        P(None, "tensor", None),
        P(),
        P(None, None, "tensor"),
        P(None, "tensor"),
        P(None, "tensor", None),
        P(),
        P(None, None, "tensor"),
        P(None, "tensor"),
    )
    out_specs = (
        P("dp", None, None),
        P("dp", None, None),
        P("dp", None),
        P(None, "dp", None, "tensor"),
        P(None, None, "tensor"),
        P(None, "tensor", "dp"),
        P(),
        P(None, "dp", "tensor"),
        P(None, "tensor"),
        P(None, "tensor", "dp"),
        P(),
        P(None, "dp", "tensor"),
        P(None, "tensor"),
    )
    return jax.shard_map(
        on_device, mesh=mesh, in_specs=in_specs, out_specs=out_specs, check_vma=False
    )
```

profile of v0, /device:TPU:0, one launch (start us, length us, event | category | flops | bytes accessed | tf_op | source)
XLA Modules:
  0.0 574.5 jit_solution(8802800314265596121)
XLA Ops:
  2.7 5.8 %fusion.2 = (f32[2304]{0:T(1024)S(1)}, f32[2304]{0:T(1024)S(1)}) fusion(f32[2,768,2304]{2,1,0:T(8,128)} %param.24, f32[768]{0:T(1024)S(1)} %multiply_reduce_fusion.20), kind=kLoop, calls=%fused_computation.6 | loop fusion | flops 7073280 | bytes 14177280 | tf_op jit(solution)/shard_map/reduce_sum | solution.py:45
  14.8 4.0 fusion.62
  26.7 15.8 %collective-permute-done.1 = f32[1,256,768]{2,1,0:T(8,128)S(1)} collective-permute-done((f32[1,256,768]{2,1,0:T(8,128)S(1)}, f32[1,256,768]{2,1,0:T(8,128)S(1)}, u32[]{:S(2)}, u32[]{:S(2)}) %collective-permute-start.1) | collective-permute-done | bytes 786464 | tf_op jit(solution)/shard_map/ppermute | solution.py:29
  44.2 4.7 fusion.40
  48.9 5.5 fusion.77
  59.7 13.0 %collective-permute-done.2 = f32[1,256,768]{2,1,0:T(8,128)} collective-permute-done((f32[1,256,768]{2,1,0:T(8,128)S(1)}, f32[1,256,768]{2,1,0:T(8,128)}, u32[]{:S(2)}, u32[]{:S(2)}) %collective-permute-start.2) | collective-permute-done | bytes 786464 | tf_op jit(solution)/shard_map/ppermute | solution.py:29
  74.9 15.7 %fusion.65 = f32[1,256,3,384]{3,1,2,0:T(8,128)S(1)} fusion(f32[2,768,3,384]{3,1,2,0:T(8,128)} %param.16, f32[1,256,768]{2,1,0:T(8,128)S(1)} %get-tuple-element.127, f32[768]{0:T(1024)S(1)} %copy-done.114, f32[768]{0:T(1024)S(1)} %copy-done.96, f32[256]{0:T(256)S(1)} %fusion.180, f32[256]{0:T(256)S(1)} %broadcast_multiply_fusion.1), kind=kOutput, calls=%fused_computation.81 | convolution fusion | flops 1359740928 | bytes 5513216 | tf_op jit(solution)/shard_map/bsd,dcm->bscm/dot_general | solution.py:126
  102.2 21.9 %all-gather.2 = f32[16,1,768]{2,1,0:T(1,128)S(1)} all-gather(f32[1,1,768]{2,1,0:T(1,128)} %get-tuple-element.100), channel_id=1, replica_groups=mesh['dp'=16,'tensor'=2] {'dp'}, dimensions={0}, use_global_device_ids=true | all-gather | bytes 52224 | tf_op jit(solution)/shard_map/all_gather | solution.py:118
  126.3 4.9 fusion.43
  131.3 6.3 %fusion.206 = (f32[1536]{0:T(1024)}, f32[256,1536]{1,0:T(8,128)S(1)}) fusion(f32[256,1536]{1,0:T(8,128)S(1)} %fusion.43, f32[2,1536,768]{2,1,0:T(8,128)} %param.22, f32[1,256,768]{2,1,0:T(8,128)S(1)} %copy-done.64, f32[768]{0:T(1024)S(1)} %copy-done.154), kind=kOutput, calls=%fused_computation.396 | convolution fusion | flops 1819998720 | bytes 8659968 | tf_op jit(solution)/shard_map/bsd,fd->bsf/dot_general | solution.py:197
  142.9 5.6 fusion.83
  150.5 11.1 %collective-permute-done.5 = f32[1,256,768]{2,1,0:T(8,128)} collective-permute-done((f32[1,256,768]{2,1,0:T(8,128)}, f32[1,256,768]{2,1,0:T(8,128)}, u32[]{:S(2)}, u32[]{:S(2)}) %collective-permute-start.5) | collective-permute-done | bytes 786464 | tf_op jit(solution)/shard_map/ppermute | solution.py:29
  163.9 13.8 %collective-permute-done.4 = f32[1,256,768]{2,1,0:T(8,128)S(1)} collective-permute-done((f32[1,256,768]{2,1,0:T(8,128)S(1)}, f32[1,256,768]{2,1,0:T(8,128)S(1)}, u32[]{:S(2)}, u32[]{:S(2)}) %collective-permute-start.4) | collective-permute-done | bytes 786464 | tf_op jit(solution)/shard_map/ppermute | solution.py:29
  191.5 4.7 fusion.71
  230.6 6.0 %fusion.207 = (f32[1536]{0:T(1024)}, f32[256,1536]{1,0:T(8,128)S(1)}) fusion(f32[256,1536]{1,0:T(8,128)S(1)} %copy-done.7, f32[2,1536,768]{2,1,0:T(8,128)} %param.22, f32[1,256,768]{2,1,0:T(8,128)S(1)} %get-tuple-element.168, f32[768]{0:T(1024)S(1)} %copy-done.92), kind=kOutput, calls=%fused_computation.397 | convolution fusion | flops 1819998720 | bytes 8659968 | tf_op jit(solution)/shard_map/bsd,fd->bsf/dot_general | solution.py:197
  246.0 21.6 %all-gather.1 = f32[16,1,6528]{2,1,0:T(1,128)} all-gather(f32[1,1,6528]{2,1,0:T(1,128)S(1)} %maximum_bitcast_fusion.1), channel_id=1, replica_groups=mesh['dp'=16,'tensor'=2] {'dp'}, dimensions={0}, use_global_device_ids=true | all-gather | bytes 443904 | tf_op jit(solution)/shard_map/all_gather | solution.py:248
  293.6 5.0 collective-permute-done.25
  312.0 4.8 fusion.68
  330.7 5.6 collective-permute-done.8
  341.4 18.7 %all-gather = f32[16,1,6528]{2,1,0:T(1,128)S(1)} all-gather(f32[1,1,6528]{2,1,0:T(1,128)S(1)} %maximum_bitcast_fusion), channel_id=1, replica_groups=mesh['dp'=16,'tensor'=2] {'dp'}, dimensions={0}, use_global_device_ids=true | all-gather | bytes 443904 | tf_op jit(solution)/shard_map/all_gather | solution.py:248
  361.2 5.9 %fusion.3 = (f32[768]{0:T(1024)S(1)}, f32[768]{0:T(1024)S(1)}) fusion(f32[2,768,2304]{2,1,0:T(8,128)} %param.24, f32[2304]{0:T(1024)S(1)} %get-tuple-element.110, f32[2304]{0:T(1024)S(1)} %copy-done.100), kind=kLoop, calls=%fused_computation.7 | loop fusion | flops 7076352 | bytes 14180352 | tf_op jit(solution)/shard_map/reduce_sum | solution.py:51
  394.1 5.7 collective-permute-done.21
  405.8 29.7 %collective-permute-done.15 = f32[4,48,1152]{2,1,0:T(8,128)S(1)} collective-permute-done((f32[4,48,1152]{2,1,0:T(8,128)S(1)}, f32[4,48,1152]{2,1,0:T(8,128)S(1)}, u32[]{:S(2)}, u32[]{:S(2)}) %collective-permute-start.15) | collective-permute-done | bytes 884768 | tf_op jit(solution)/shard_map/ppermute | solution.py:85
  436.5 24.4 %collective-permute-done.31 = f32[4,48,1536]{2,1,0:T(8,128)S(1)} collective-permute-done((f32[4,48,1536]{2,1,0:T(8,128)S(1)}, f32[4,48,1536]{2,1,0:T(8,128)S(1)}, u32[]{:S(2)}, u32[]{:S(2)}) %collective-permute-start.31) | collective-permute-done | bytes 1179680 | tf_op jit(solution)/shard_map/ppermute | solution.py:85
  466.3 23.2 %collective-permute-done.17 = f32[1,48,1152]{2,1,0:T(8,128)S(1)} collective-permute-done((f32[1,48,1152]{2,1,0:T(8,128)S(1)}, f32[1,48,1152]{2,1,0:T(8,128)S(1)}, u32[]{:S(2)}, u32[]{:S(2)}) %collective-permute-start.17) | collective-permute-done | bytes 221216 | tf_op jit(solution)/shard_map/ppermute | solution.py:85
  497.9 13.5 %collective-permute-done.41 = f32[1,48,1536]{2,1,0:T(8,128)S(1)} collective-permute-done((f32[1,48,1536]{2,1,0:T(8,128)S(1)}, f32[1,48,1536]{2,1,0:T(8,128)S(1)}, u32[]{:S(2)}, u32[]{:S(2)}) %collective-permute-start.41) | collective-permute-done | bytes 294944 | tf_op jit(solution)/shard_map/ppermute | solution.py:85
  511.4 5.5 collective-permute-done.33
  517.0 3.6 collective-permute-done.36
  520.7 13.3 %collective-permute-done.11 = f32[4,48,1152]{2,1,0:T(8,128)S(1)} collective-permute-done((f32[4,48,1152]{2,1,0:T(8,128)S(1)}, f32[4,48,1152]{2,1,0:T(8,128)S(1)}, u32[]{:S(2)}, u32[]{:S(2)}) %collective-permute-start.11) | collective-permute-done | bytes 884768 | tf_op jit(solution)/shard_map/ppermute | solution.py:85
  537.4 12.3 %collective-permute-done.12 = f32[2,48,1152]{2,1,0:T(8,128)S(1)} collective-permute-done((f32[2,48,1152]{2,1,0:T(8,128)S(1)}, f32[2,48,1152]{2,1,0:T(8,128)S(1)}, u32[]{:S(2)}, u32[]{:S(2)}) %collective-permute-start.12) | collective-permute-done | bytes 442400 | tf_op jit(solution)/shard_map/ppermute | solution.py:85
  550.6 11.2 %collective-permute-done.28 = f32[2,48,1536]{2,1,0:T(8,128)S(1)} collective-permute-done((f32[2,48,1536]{2,1,0:T(8,128)S(1)}, f32[2,48,1536]{2,1,0:T(8,128)S(1)}, u32[]{:S(2)}, u32[]{:S(2)}) %collective-permute-start.28) | collective-permute-done | bytes 589856 | tf_op jit(solution)/shard_map/ppermute | solution.py:85
  564.1 9.4 %collective-permute-done.29 = f32[1,48,1536]{2,1,0:T(8,128)S(1)} collective-permute-done((f32[1,48,1536]{2,1,0:T(8,128)S(1)}, f32[1,48,1536]{2,1,0:T(8,128)S(1)}, u32[]{:S(2)}, u32[]{:S(2)}) %collective-permute-start.29) | collective-permute-done | bytes 294944 | tf_op jit(solution)/shard_map/ppermute | solution.py:85
  (673 shorter events, 219.0 us)
Async XLA Ops:
  23.4 19.1 %collective-permute-start.1 = (f32[1,256,768]{2,1,0:T(8,128)S(1)}, f32[1,256,768]{2,1,0:T(8,128)S(1)}, u32[]{:S(2)}, u32[]{:S(2)}) collective-permute-start(f32[1,256,768]{2,1,0:T(8,128)S(1)} %convolution_bitcast_fusion.3), channel_id=1, source_target_pairs={{0,1},{1,0},{2,3},{3,2},{4,5},{5,4},{6,7},{7,6},{8,9},{9,8},{10,11... | collective-permute-start | bytes 2359304 | tf_op jit(solution)/shard_map/ppermute | solution.py:29
  54.4 18.3 %collective-permute-start.2 = (f32[1,256,768]{2,1,0:T(8,128)S(1)}, f32[1,256,768]{2,1,0:T(8,128)}, u32[]{:S(2)}, u32[]{:S(2)}) collective-permute-start(f32[1,256,768]{2,1,0:T(8,128)S(1)} %fusion.77), channel_id=1, source_target_pairs={{0,1},{1,0},{2,3},{3,2},{4,5},{5,4},{6,7},{7,6},{8,9},{9,8},{10,11... | collective-permute-start | bytes 2359304 | tf_op jit(solution)/shard_map/ppermute | solution.py:29
  101.9 22.2 %collective-permute-start.3 = (f32[1,256,768]{2,1,0:T(8,128)}, f32[1,256,768]{2,1,0:T(8,128)}, u32[]{:S(2)}, u32[]{:S(2)}) collective-permute-start(f32[1,256,768]{2,1,0:T(8,128)} %convolution_bitcast_fusion.2), channel_id=1, source_target_pairs={{0,1},{1,0},{2,3},{3,2},{4,5},{5,4},{6,7},{7,6},{8,9},{9,8},{10,11... | collective-permute-start | bytes 2359304 | tf_op jit(solution)/shard_map/ppermute | solution.py:29
  140.9 20.7 %collective-permute-start.5 = (f32[1,256,768]{2,1,0:T(8,128)}, f32[1,256,768]{2,1,0:T(8,128)}, u32[]{:S(2)}, u32[]{:S(2)}) collective-permute-start(f32[1,256,768]{2,1,0:T(8,128)} %fusion.80), channel_id=1, source_target_pairs={{0,1},{1,0},{2,3},{3,2},{4,5},{5,4},{6,7},{7,6},{8,9},{9,8},{10,11... | collective-permute-start | bytes 2359304 | tf_op jit(solution)/shard_map/ppermute | solution.py:29
  148.5 29.3 %collective-permute-start.4 = (f32[1,256,768]{2,1,0:T(8,128)S(1)}, f32[1,256,768]{2,1,0:T(8,128)S(1)}, u32[]{:S(2)}, u32[]{:S(2)}) collective-permute-start(f32[1,256,768]{2,1,0:T(8,128)S(1)} %fusion.83), channel_id=1, source_target_pairs={{0,1},{1,0},{2,3},{3,2},{4,5},{5,4},{6,7},{7,6},{8,9},{9,8},{10,11... | collective-permute-start | bytes 2359304 | tf_op jit(solution)/shard_map/ppermute | solution.py:29
  196.2 27.9 %collective-permute-start.6 = (f32[1,256,768]{2,1,0:T(8,128)}, f32[1,256,768]{2,1,0:T(8,128)}, u32[]{:S(2)}, u32[]{:S(2)}) collective-permute-start(f32[1,256,768]{2,1,0:T(8,128)} %fusion.71), channel_id=1, source_target_pairs={{0,1},{1,0},{2,3},{3,2},{4,5},{5,4},{6,7},{7,6},{8,9},{9,8},{10,11... | collective-permute-start | bytes 2359304 | tf_op jit(solution)/shard_map/ppermute | solution.py:29
  214.0 163.1 %collective-permute-start.38 = (f32[384,1536]{1,0:T(8,128)}, f32[384,1536]{1,0:T(8,128)}, u32[]{:S(2)}, u32[]{:S(2)}) collective-permute-start(f32[384,1536]{1,0:T(8,128)} %fusion.187), channel_id=1, source_target_pairs={{0,2},{2,0},{4,6},{6,4},{8,10},{10,8},{12,14},{14,12},{16,18},{18,... | collective-permute-start | bytes 7077896 | tf_op jit(solution)/shard_map/ppermute | solution.py:75
  221.5 160.6 %collective-permute-start.30 = (f32[384,1536]{1,0:T(8,128)}, f32[384,1536]{1,0:T(8,128)}, u32[]{:S(2)}, u32[]{:S(2)}) collective-permute-start(f32[384,1536]{1,0:T(8,128)} %fusion.215), channel_id=1, source_target_pairs={{0,2},{2,0},{4,6},{6,4},{8,10},{10,8},{12,14},{14,12},{16,18},{18,... | collective-permute-start | bytes 7077896 | tf_op jit(solution)/shard_map/ppermute | solution.py:75
  224.1 59.1 %collective-permute-start.23 = (f32[4,48,384]{2,1,0:T(8,128)}, f32[4,48,384]{2,1,0:T(8,128)}, u32[]{:S(2)}, u32[]{:S(2)}) collective-permute-start(f32[4,48,384]{2,1,0:T(8,128)} %dynamic-slice_bitcast_fusion.12), channel_id=1, source_target_pairs={{0,4},{2,6},{4,0},{6,2},{8,12},{10,14},{12,8},{14,10},{16,20},{18,... | collective-permute-start | bytes 884744 | tf_op jit(solution)/shard_map/ppermute | solution.py:85
  240.0 59.3 %collective-permute-start.7 = (f32[1,256,768]{2,1,0:T(8,128)}, f32[1,256,768]{2,1,0:T(8,128)}, u32[]{:S(2)}, u32[]{:S(2)}) collective-permute-start(f32[1,256,768]{2,1,0:T(8,128)} %fusion.74), channel_id=1, source_target_pairs={{0,1},{1,0},{2,3},{3,2},{4,5},{5,4},{6,7},{7,6},{8,9},{9,8},{10,11... | collective-permute-start | bytes 2359304 | tf_op jit(solution)/shard_map/ppermute | solution.py:29
  286.3 115.7 %collective-permute-start.34 = (f32[384,1536]{1,0:T(8,128)}, f32[384,1536]{1,0:T(8,128)}, u32[]{:S(2)}, u32[]{:S(2)}) collective-permute-start(f32[384,1536]{1,0:T(8,128)} %fusion.186), channel_id=1, source_target_pairs={{0,2},{2,0},{4,6},{6,4},{8,10},{10,8},{12,14},{14,12},{16,18},{18,... | collective-permute-start | bytes 7077896 | tf_op jit(solution)/shard_map/ppermute | solution.py:75
  316.8 19.5 %collective-permute-start.8 = (f32[1,256,768]{2,1,0:T(8,128)}, f32[1,256,768]{2,1,0:T(8,128)}, u32[]{:S(2)}, u32[]{:S(2)}) collective-permute-start(f32[1,256,768]{2,1,0:T(8,128)} %fusion.68), channel_id=1, source_target_pairs={{0,1},{1,0},{2,3},{3,2},{4,5},{5,4},{6,7},{7,6},{8,9},{9,8},{10,11... | collective-permute-start | bytes 2359304 | tf_op jit(solution)/shard_map/ppermute | solution.py:29
  328.5 59.8 %collective-permute-start.14 = (f32[384,1152]{1,0:T(8,128)}, f32[384,1152]{1,0:T(8,128)}, u32[]{:S(2)}, u32[]{:S(2)}) collective-permute-start(f32[384,1152]{1,0:T(8,128)} %fusion.211), channel_id=1, source_target_pairs={{0,2},{2,0},{4,6},{6,4},{8,10},{10,8},{12,14},{14,12},{16,18},{18,... | collective-permute-start | bytes 5308424 | tf_op jit(solution)/shard_map/ppermute | solution.py:75
  336.2 127.0 %collective-permute-start.26 = (f32[384,1536]{1,0:T(8,128)}, f32[384,1536]{1,0:T(8,128)}, u32[]{:S(2)}, u32[]{:S(2)}) collective-permute-start(f32[384,1536]{1,0:T(8,128)} %fusion.214), channel_id=1, source_target_pairs={{0,2},{2,0},{4,6},{6,4},{8,10},{10,8},{12,14},{14,12},{16,18},{18,... | collective-permute-start | bytes 7077896 | tf_op jit(solution)/shard_map/ppermute | solution.py:75
  386.6 107.3 %collective-permute-start.10 = (f32[384,1152]{1,0:T(8,128)S(1)}, f32[384,1152]{1,0:T(8,128)S(1)}, u32[]{:S(2)}, u32[]{:S(2)}) collective-permute-start(f32[384,1152]{1,0:T(8,128)S(1)} %fusion.210), channel_id=1, source_target_pairs={{0,2},{2,0},{4,6},{6,4},{8,10},{10,8},{12,14},{14,12},{16,18},{18,... | collective-permute-start | bytes 5308424 | tf_op jit(solution)/shard_map/ppermute | solution.py:75
  387.7 48.4 %collective-permute-start.39 = (f32[4,48,1536]{2,1,0:T(8,128)S(1)}, f32[4,48,1536]{2,1,0:T(8,128)S(1)}, u32[]{:S(2)}, u32[]{:S(2)}) collective-permute-start(f32[4,48,1536]{2,1,0:T(8,128)S(1)} %dynamic-slice_bitcast_fusion), channel_id=1, source_target_pairs={{0,4},{2,6},{4,0},{6,2},{8,12},{10,14},{12,8},{14,10},{16,20},{18,... | collective-permute-start | bytes 3538952 | tf_op jit(solution)/shard_map/ppermute | solution.py:85
  399.8 35.8 %collective-permute-start.15 = (f32[4,48,1152]{2,1,0:T(8,128)S(1)}, f32[4,48,1152]{2,1,0:T(8,128)S(1)}, u32[]{:S(2)}, u32[]{:S(2)}) collective-permute-start(f32[4,48,1152]{2,1,0:T(8,128)S(1)} %dynamic-slice_bitcast_fusion.4), channel_id=1, source_target_pairs={{0,4},{2,6},{4,0},{6,2},{8,12},{10,14},{12,8},{14,10},{16,20},{18,... | collective-permute-start | bytes 2654216 | tf_op jit(solution)/shard_map/ppermute | solution.py:85
  402.0 58.8 %collective-permute-start.31 = (f32[4,48,1536]{2,1,0:T(8,128)S(1)}, f32[4,48,1536]{2,1,0:T(8,128)S(1)}, u32[]{:S(2)}, u32[]{:S(2)}) collective-permute-start(f32[4,48,1536]{2,1,0:T(8,128)S(1)} %dynamic-slice_bitcast_fusion.2), channel_id=1, source_target_pairs={{0,4},{2,6},{4,0},{6,2},{8,12},{10,14},{12,8},{14,10},{16,20},{18,... | collective-permute-start | bytes 3538952 | tf_op jit(solution)/shard_map/ppermute | solution.py:85
  435.5 61.1 %collective-permute-start.35 = (f32[4,48,1536]{2,1,0:T(8,128)S(1)}, f32[4,48,1536]{2,1,0:T(8,128)S(1)}, u32[]{:S(2)}, u32[]{:S(2)}) collective-permute-start(f32[4,48,1536]{2,1,0:T(8,128)S(1)} %dynamic-slice_bitcast_fusion.1), channel_id=1, source_target_pairs={{0,4},{2,6},{4,0},{6,2},{8,12},{10,14},{12,8},{14,10},{16,20},{18,... | collective-permute-start | bytes 3538952 | tf_op jit(solution)/shard_map/ppermute | solution.py:85
  436.2 24.9 %collective-permute-start.16 = (f32[2,48,1152]{2,1,0:T(8,128)S(1)}, f32[2,48,1152]{2,1,0:T(8,128)S(1)}, u32[]{:S(2)}, u32[]{:S(2)}) collective-permute-start(f32[2,48,1152]{2,1,0:T(8,128)S(1)} %dynamic-slice_bitcast_fusion.10), channel_id=1, source_target_pairs={{0,8},{2,10},{4,12},{6,14},{8,0},{10,2},{12,4},{14,6},{16,24},{18,... | collective-permute-start | bytes 1327112 | tf_op jit(solution)/shard_map/ppermute | solution.py:85
  460.8 29.2 %collective-permute-start.40 = (f32[2,48,1536]{2,1,0:T(8,128)S(1)}, f32[2,48,1536]{2,1,0:T(8,128)S(1)}, u32[]{:S(2)}, u32[]{:S(2)}) collective-permute-start(f32[2,48,1536]{2,1,0:T(8,128)S(1)} %dynamic-slice_bitcast_fusion.6), channel_id=1, source_target_pairs={{0,8},{2,10},{4,12},{6,14},{8,0},{10,2},{12,4},{14,6},{16,24},{18,... | collective-permute-start | bytes 1769480 | tf_op jit(solution)/shard_map/ppermute | solution.py:85
  461.0 32.7 %collective-permute-start.32 = (f32[2,48,1536]{2,1,0:T(8,128)S(1)}, f32[2,48,1536]{2,1,0:T(8,128)S(1)}, u32[]{:S(2)}, u32[]{:S(2)}) collective-permute-start(f32[2,48,1536]{2,1,0:T(8,128)S(1)} %dynamic-slice_bitcast_fusion.8), channel_id=1, source_target_pairs={{0,8},{2,10},{4,12},{6,14},{8,0},{10,2},{12,4},{14,6},{16,24},{18,... | collective-permute-start | bytes 1769480 | tf_op jit(solution)/shard_map/ppermute | solution.py:85
  463.2 26.3 %collective-permute-start.17 = (f32[1,48,1152]{2,1,0:T(8,128)S(1)}, f32[1,48,1152]{2,1,0:T(8,128)S(1)}, u32[]{:S(2)}, u32[]{:S(2)}) collective-permute-start(f32[1,48,1152]{2,1,0:T(8,128)S(1)} %constant_dynamic-slice_fusion.19), channel_id=1, source_target_pairs={{0,16},{2,18},{4,20},{6,22},{8,24},{10,26},{12,28},{14,30},{16,0},... | collective-permute-start | bytes 663560 | tf_op jit(solution)/shard_map/ppermute | solution.py:85
  489.5 46.0 %collective-permute-start.27 = (f32[4,48,1536]{2,1,0:T(8,128)S(1)}, f32[4,48,1536]{2,1,0:T(8,128)S(1)}, u32[]{:S(2)}, u32[]{:S(2)}) collective-permute-start(f32[4,48,1536]{2,1,0:T(8,128)S(1)} %dynamic-slice_bitcast_fusion.3), channel_id=1, source_target_pairs={{0,4},{2,6},{4,0},{6,2},{8,12},{10,14},{12,8},{14,10},{16,20},{18,... | collective-permute-start | bytes 3538952 | tf_op jit(solution)/shard_map/ppermute | solution.py:85
  490.2 21.2 %collective-permute-start.41 = (f32[1,48,1536]{2,1,0:T(8,128)S(1)}, f32[1,48,1536]{2,1,0:T(8,128)S(1)}, u32[]{:S(2)}, u32[]{:S(2)}) collective-permute-start(f32[1,48,1536]{2,1,0:T(8,128)S(1)} %constant_dynamic-slice_fusion.1), channel_id=1, source_target_pairs={{0,16},{2,18},{4,20},{6,22},{8,24},{10,26},{12,28},{14,30},{16,0},... | collective-permute-start | bytes 884744 | tf_op jit(solution)/shard_map/ppermute | solution.py:85
  493.8 23.1 %collective-permute-start.33 = (f32[1,48,1536]{2,1,0:T(8,128)S(1)}, f32[1,48,1536]{2,1,0:T(8,128)S(1)}, u32[]{:S(2)}, u32[]{:S(2)}) collective-permute-start(f32[1,48,1536]{2,1,0:T(8,128)S(1)} %constant_dynamic-slice_fusion.7), channel_id=1, source_target_pairs={{0,16},{2,18},{4,20},{6,22},{8,24},{10,26},{12,28},{14,30},{16,0},... | collective-permute-start | bytes 884744 | tf_op jit(solution)/shard_map/ppermute | solution.py:85
  495.0 39.0 %collective-permute-start.11 = (f32[4,48,1152]{2,1,0:T(8,128)S(1)}, f32[4,48,1152]{2,1,0:T(8,128)S(1)}, u32[]{:S(2)}, u32[]{:S(2)}) collective-permute-start(f32[4,48,1152]{2,1,0:T(8,128)S(1)} %dynamic-slice_bitcast_fusion.5), channel_id=1, source_target_pairs={{0,4},{2,6},{4,0},{6,2},{8,12},{10,14},{12,8},{14,10},{16,20},{18,... | collective-permute-start | bytes 2654216 | tf_op jit(solution)/shard_map/ppermute | solution.py:85
  496.8 23.7 %collective-permute-start.36 = (f32[2,48,1536]{2,1,0:T(8,128)S(1)}, f32[2,48,1536]{2,1,0:T(8,128)S(1)}, u32[]{:S(2)}, u32[]{:S(2)}) collective-permute-start(f32[2,48,1536]{2,1,0:T(8,128)S(1)} %dynamic-slice_bitcast_fusion.7), channel_id=1, source_target_pairs={{0,8},{2,10},{4,12},{6,14},{8,0},{10,2},{12,4},{14,6},{16,24},{18,... | collective-permute-start | bytes 1769480 | tf_op jit(solution)/shard_map/ppermute | solution.py:85
  520.7 15.8 %collective-permute-start.37 = (f32[1,48,1536]{2,1,0:T(8,128)S(1)}, f32[1,48,1536]{2,1,0:T(8,128)S(1)}, u32[]{:S(2)}, u32[]{:S(2)}) collective-permute-start(f32[1,48,1536]{2,1,0:T(8,128)S(1)} %constant_dynamic-slice_fusion.4), channel_id=1, source_target_pairs={{0,16},{2,18},{4,20},{6,22},{8,24},{10,26},{12,28},{14,30},{16,0},... | collective-permute-start | bytes 884744 | tf_op jit(solution)/shard_map/ppermute | solution.py:85
  534.1 15.5 %collective-permute-start.12 = (f32[2,48,1152]{2,1,0:T(8,128)S(1)}, f32[2,48,1152]{2,1,0:T(8,128)S(1)}, u32[]{:S(2)}, u32[]{:S(2)}) collective-permute-start(f32[2,48,1152]{2,1,0:T(8,128)S(1)} %dynamic-slice_bitcast_fusion.11), channel_id=1, source_target_pairs={{0,8},{2,10},{4,12},{6,14},{8,0},{10,2},{12,4},{14,6},{16,24},{18,... | collective-permute-start | bytes 1327112 | tf_op jit(solution)/shard_map/ppermute | solution.py:85
  535.7 26.0 %collective-permute-start.28 = (f32[2,48,1536]{2,1,0:T(8,128)S(1)}, f32[2,48,1536]{2,1,0:T(8,128)S(1)}, u32[]{:S(2)}, u32[]{:S(2)}) collective-permute-start(f32[2,48,1536]{2,1,0:T(8,128)S(1)} %dynamic-slice_bitcast_fusion.9), channel_id=1, source_target_pairs={{0,8},{2,10},{4,12},{6,14},{8,0},{10,2},{12,4},{14,6},{16,24},{18,... | collective-permute-start | bytes 1769480 | tf_op jit(solution)/shard_map/ppermute | solution.py:85
  549.8 13.4 %collective-permute-start.13 = (f32[1,48,1152]{2,1,0:T(8,128)S(1)}, f32[1,48,1152]{2,1,0:T(8,128)S(1)}, u32[]{:S(2)}, u32[]{:S(2)}) collective-permute-start(f32[1,48,1152]{2,1,0:T(8,128)S(1)} %constant_dynamic-slice_fusion.22), channel_id=1, source_target_pairs={{0,16},{2,18},{4,20},{6,22},{8,24},{10,26},{12,28},{14,30},{16,0},... | collective-permute-start | bytes 663560 | tf_op jit(solution)/shard_map/ppermute | solution.py:85
  (192 other events, 1133.6 us)
where the time goes:
time: 585 us; the launch traced here: 575 us
  waiting for transfers between devices  222 us (38%)
  matrix products  126 us (22%)
  local copies, waits for them, and re-layouts  68.9 us (12%)
  blocking collectives  62.3 us (11%)
  other arithmetic  58.5 us (10%)
  starting transfers between devices  33 us (6%)
    ppermute x24, waiting for transfers between devices, scattered_grad(): total = kept + lax.ppermute(away, 'dp', pairs)  163 us
    ppermute x9, waiting for transfers between devices, pair_sum(): return value + lax.ppermute(value, 'tensor', [(0, 1), (1, 0)])  59.2 us
    all_gather x2, blocking collectives, on_device(): lax.all_gather(jnp.concatenate([own_cols, line], axis=1), 'dp', axis=0, t...  40.3 us
    dot_general x16, matrix products, product(): return jnp.dot(chosen.reshape(rows // 2, tokens), right, precision=high)  35.7 us
    all_gather x1, blocking collectives, on_device(): activated_all = lax.all_gather(activated, 'dp', axis=0, tiled=True)  21.9 us
    dot_general x2, matrix products, on_device(): jnp.einsum('bsd,dcm->bscm', modul_a, w_qkv[layer_index], precision=high)  19.6 us
    ppermute x24, starting transfers between devices, scattered_grad(): total = kept + lax.ppermute(away, 'dp', pairs)  18.2 us
    transpose x8, local copies, waits for them, and re-layouts, scattered_grad(): left_t = left.reshape(tokens, rows).T  15.7 us
  transfers between devices with their start and end apart: 42, of which 19 were waited for; matrix products, arithmetic and copies ran while one was open for 27% of the time, Pallas kernels for 0%

commit v1 on v0

--- a/solution.py
+++ b/solution.py
@@ -6,6 +6,18 @@
 HEAD_DIM = 64
 high = lax.Precision.HIGH
 eps_norm = 1e-06
+
+
+def collect(x, axis, dim):
+    ways, here, turn = (lax.axis_size(axis), lax.axis_index(axis), x.shape[dim])
+    line, have = (x, 1)
+    while have < ways:
+        line = jnp.concatenate(
+            [line, lax.ppermute(line, axis, [(d, (d - have) % ways) for d in range(ways)])],
+            axis=dim,
+        )
+        have = 2 * have
+    return jnp.roll(line, here * turn, axis=dim)
 
 
 def layer_norm(values):
@@ -245,9 +257,7 @@
         own_cols, biases = pieces[layer_index]
         line = jnp.concatenate(biases)[None]
         line = jnp.concatenate([line, jnp.zeros((batch - 1, line.shape[1]), line.dtype)], axis=0)
-        gathered = lax.all_gather(
-            jnp.concatenate([own_cols, line], axis=1), "dp", axis=0, tiled=True
-        )
+        gathered = collect(jnp.concatenate([own_cols, line], axis=1), "dp", 0)
         mod_grads[layer_index] = jnp.einsum(
             "bd,bm->dm", activated_rows, gathered[:, :mod_cols], precision=high
         )

time: 585 us -> 640 us (1.094)
  waiting for transfers between devices: 222 us -> 321 us
  blocking collectives: 62.3 us -> 20.7 us
  matrix products: 126 us -> 115 us
  starting transfers between devices: 33 us -> 43.8 us
    ppermute x24, waiting for transfers between devices: 163 us -> 223 us  [scattered_grad(): total = kept + lax.ppermute(away, 'dp', pairs)]
    all_gather x2 -> x0, blocking collectives: 40.3 us -> none  [on_device(): lax.all_gather(jnp.concatenate([own_cols, line], axis=1), 'dp', axis=0, t...]
    ppermute x0 -> x8, waiting for transfers between devices: none -> 22.7 us  [collect(): lax.ppermute(line, axis, [(d, (d - have) % ways) for d in range(ways)])]
    ppermute x9, waiting for transfers between devices: 59.2 us -> 75.1 us  [pair_sum(): return value + lax.ppermute(value, 'tensor', [(0, 1), (1, 0)])]
    dot_general x2, matrix products: 19.6 us -> 8.16 us  [on_device(): jnp.einsum('bsd,dcm->bscm', modul_a, w_qkv[layer_index], precision=high)]
    ppermute x0 -> x8, starting transfers between devices: none -> 9.27 us  [collect(): lax.ppermute(line, axis, [(d, (d - have) % ways) for d in range(ways)])]
    dynamic_slice x8 -> x4, local copies, waits for them, and re-layouts: 13 us -> 6.01 us  [product(): chosen = lax.dynamic_index_in_dim(blocks, which, 1, keepdims=False)]
  transfers between devices with their start and end apart: 42 -> 50, of which waited for: 19 -> 31; matrix products, arithmetic and copies ran while one was open for 27% -> 23% of each run, Pallas kernels for 0% -> 0%
where the time goes in v1:
time: 640 us; the launch traced here: 629 us
  waiting for transfers between devices  321 us (50%)
  matrix products  115 us (18%)
  local copies, waits for them, and re-layouts  67.4 us (11%)
  other arithmetic  57.5 us (9%)
  starting transfers between devices  43.8 us (7%)
  blocking collectives  20.7 us (3%)
    ppermute x24, waiting for transfers between devices, scattered_grad(): total = kept + lax.ppermute(away, 'dp', pairs)  223 us
    ppermute x9, waiting for transfers between devices, pair_sum(): return value + lax.ppermute(value, 'tensor', [(0, 1), (1, 0)])  75.1 us
    dot_general x16, matrix products, product(): return jnp.dot(chosen.reshape(rows // 2, tokens), right, precision=high)  33.3 us
    ppermute x8, waiting for transfers between devices, collect(): lax.ppermute(line, axis, [(d, (d - have) % ways) for d in range(ways)])  22.7 us
    ppermute x24, starting transfers between devices, scattered_grad(): total = kept + lax.ppermute(away, 'dp', pairs)  21.1 us
    all_gather x1, blocking collectives, on_device(): activated_all = lax.all_gather(activated, 'dp', axis=0, tiled=True)  20.7 us
    transpose x8, local copies, waits for them, and re-layouts, scattered_grad(): left_t = left.reshape(tokens, rows).T  14.3 us
  transfers between devices with their start and end apart: 50, of which 31 were waited for; matrix products, arithmetic and copies ran while one was open for 23% of the time, Pallas kernels for 0%

profile of v1, /device:TPU:0, one launch (start us, length us, event | category | flops | bytes accessed | tf_op | source)
XLA Modules:
  0.0 628.9 jit_solution(7763291434309436591)
XLA Ops:
  2.7 5.8 fusion.2
  26.7 15.8 %collective-permute-done.1 = f32[1,256,768]{2,1,0:T(8,128)S(1)} collective-permute-done((f32[1,256,768]{2,1,0:T(8,128)S(1)}, f32[1,256,768]{2,1,0:T(8,128)S(1)}, u32[]{:S(2)}, u32[]{:S(2)}) %collective-permute-start.1) | collective-permute-done | bytes 786464 | tf_op jit(solution)/shard_map/ppermute | solution.py:41
  48.9 5.5 fusion.77
  61.9 10.7 %collective-permute-done.2 = f32[1,256,768]{2,1,0:T(8,128)} collective-permute-done((f32[1,256,768]{2,1,0:T(8,128)S(1)}, f32[1,256,768]{2,1,0:T(8,128)}, u32[]{:S(2)}, u32[]{:S(2)}) %collective-permute-start.2) | collective-permute-done | bytes 786464 | tf_op jit(solution)/shard_map/ppermute | solution.py:41
  89.4 16.9 %collective-permute-done.3 = f32[1,256,768]{2,1,0:T(8,128)S(1)} collective-permute-done((f32[1,256,768]{2,1,0:T(8,128)S(1)}, f32[1,256,768]{2,1,0:T(8,128)S(1)}, u32[]{:S(2)}, u32[]{:S(2)}) %collective-permute-start.3) | collective-permute-done | bytes 786464 | tf_op jit(solution)/shard_map/ppermute | solution.py:41
  112.3 6.3 %fusion.212 = (f32[1536]{0:T(1024)}, f32[256,1536]{1,0:T(8,128)S(1)}) fusion(f32[256,1536]{1,0:T(8,128)S(1)} %fusion.43, f32[2,1536,768]{2,1,0:T(8,128)} %param.24, f32[1,256,768]{2,1,0:T(8,128)S(1)} %copy-done.60, f32[768]{0:T(1024)S(1)} %copy-done.143), kind=kOutput, calls=%fused_computation.408 | convolution fusion | flops 1819998720 | bytes 8659968 | tf_op jit(solution)/shard_map/bsd,fd->bsf/dot_general | solution.py:209
  121.6 5.0 fusion.83
  129.6 12.2 %collective-permute-done.5 = f32[1,256,768]{2,1,0:T(8,128)S(1)} collective-permute-done((f32[1,256,768]{2,1,0:T(8,128)S(1)}, f32[1,256,768]{2,1,0:T(8,128)S(1)}, u32[]{:S(2)}, u32[]{:S(2)}) %collective-permute-start.5) | collective-permute-done | bytes 786464 | tf_op jit(solution)/shard_map/ppermute | solution.py:41
  142.8 11.7 %collective-permute-done.4 = f32[1,256,768]{2,1,0:T(8,128)S(1)} collective-permute-done((f32[1,256,768]{2,1,0:T(8,128)S(1)}, f32[1,256,768]{2,1,0:T(8,128)S(1)}, u32[]{:S(2)}, u32[]{:S(2)}) %collective-permute-start.4) | collective-permute-done | bytes 786464 | tf_op jit(solution)/shard_map/ppermute | solution.py:41
  169.3 5.0 fusion.71
  174.6 20.7 %all-gather = f32[16,1,768]{2,1,0:T(1,128)S(1)} all-gather(f32[1,1,768]{2,1,0:T(1,128)S(1)} %copy-done.145), channel_id=1, replica_groups=mesh['dp'=16,'tensor'=2] {'dp'}, dimensions={0}, use_global_device_ids=true | all-gather | bytes 52224 | tf_op jit(solution)/shard_map/all_gather | solution.py:130
  215.5 5.9 fusion.213
  221.4 6.0 fusion.74
  249.6 6.2 collective-permute-done.25
  275.4 4.9 fusion.68
  314.4 5.7 fusion.3
  330.8 7.1 %collective-permute-done.27 = f32[4,48,384]{2,1,0:T(8,128)S(1)} collective-permute-done((f32[4,48,384]{2,1,0:T(8,128)S(1)}, f32[4,48,384]{2,1,0:T(8,128)S(1)}, u32[]{:S(2)}, u32[]{:S(2)}) %collective-permute-start.27) | collective-permute-done | bytes 294944 | tf_op jit(solution)/shard_map/ppermute | solution.py:97
  338.0 6.6 %collective-permute-done.31 = f32[4,48,384]{2,1,0:T(8,128)S(1)} collective-permute-done((f32[4,48,384]{2,1,0:T(8,128)S(1)}, f32[4,48,384]{2,1,0:T(8,128)S(1)}, u32[]{:S(2)}, u32[]{:S(2)}) %collective-permute-start.31) | collective-permute-done | bytes 294944 | tf_op jit(solution)/shard_map/ppermute | solution.py:97
  350.3 5.2 collective-permute-done.28
  355.8 5.6 collective-permute-done.32
  374.9 7.8 %collective-permute-done.21 = f32[8,6528]{1,0:T(8,128)S(1)} collective-permute-done((f32[8,6528]{1,0:T(8,128)S(1)}, f32[8,6528]{1,0:T(8,128)S(1)}, u32[]{:S(2)}, u32[]{:S(2)}) %collective-permute-start.21) | collective-permute-done | bytes 208928 | tf_op jit(solution)/shard_map/ppermute | solution.py:16
  423.3 9.0 %collective-permute-done.43 = f32[4,48,1536]{2,1,0:T(8,128)S(1)} collective-permute-done((f32[4,48,1536]{2,1,0:T(8,128)S(1)}, f32[4,48,1536]{2,1,0:T(8,128)S(1)}, u32[]{:S(2)}, u32[]{:S(2)}) %collective-permute-start.43) | collective-permute-done | bytes 1179680 | tf_op jit(solution)/shard_map/ppermute | solution.py:97
  434.0 23.6 %collective-permute-done.47 = f32[4,48,1536]{2,1,0:T(8,128)S(1)} collective-permute-done((f32[4,48,1536]{2,1,0:T(8,128)S(1)}, f32[4,48,1536]{2,1,0:T(8,128)S(1)}, u32[]{:S(2)}, u32[]{:S(2)}) %collective-permute-start.47) | collective-permute-done | bytes 1179680 | tf_op jit(solution)/shard_map/ppermute | solution.py:97
  457.8 13.3 %collective-permute-done.44 = f32[2,48,1536]{2,1,0:T(8,128)S(1)} collective-permute-done((f32[2,48,1536]{2,1,0:T(8,128)S(1)}, f32[2,48,1536]{2,1,0:T(8,128)S(1)}, u32[]{:S(2)}, u32[]{:S(2)}) %collective-permute-start.44) | collective-permute-done | bytes 589856 | tf_op jit(solution)/shard_map/ppermute | solution.py:97
  471.5 12.3 %collective-permute-done.48 = f32[2,48,1536]{2,1,0:T(8,128)S(1)} collective-permute-done((f32[2,48,1536]{2,1,0:T(8,128)S(1)}, f32[2,48,1536]{2,1,0:T(8,128)S(1)}, u32[]{:S(2)}, u32[]{:S(2)}) %collective-permute-start.48) | collective-permute-done | bytes 589856 | tf_op jit(solution)/shard_map/ppermute | solution.py:97
  484.2 43.0 %collective-permute-done.11 = f32[4,48,1152]{2,1,0:T(8,128)S(1)} collective-permute-done((f32[4,48,1152]{2,1,0:T(8,128)S(1)}, f32[4,48,1152]{2,1,0:T(8,128)S(1)}, u32[]{:S(2)}, u32[]{:S(2)}) %collective-permute-start.11) | collective-permute-done | bytes 884768 | tf_op jit(solution)/shard_map/ppermute | solution.py:97
  527.3 17.9 %collective-permute-done.15 = f32[4,48,1152]{2,1,0:T(8,128)S(1)} collective-permute-done((f32[4,48,1152]{2,1,0:T(8,128)S(1)}, f32[4,48,1152]{2,1,0:T(8,128)S(1)}, u32[]{:S(2)}, u32[]{:S(2)}) %collective-permute-start.15) | collective-permute-done | bytes 884768 | tf_op jit(solution)/shard_map/ppermute | solution.py:97
  550.9 7.3 %collective-permute-done.12 = f32[2,48,1152]{2,1,0:T(8,128)S(1)} collective-permute-done((f32[2,48,1152]{2,1,0:T(8,128)S(1)}, f32[2,48,1152]{2,1,0:T(8,128)S(1)}, u32[]{:S(2)}, u32[]{:S(2)}) %collective-permute-start.12) | collective-permute-done | bytes 442400 | tf_op jit(solution)/shard_map/ppermute | solution.py:97
  558.4 14.1 %collective-permute-done.16 = f32[2,48,1152]{2,1,0:T(8,128)S(1)} collective-permute-done((f32[2,48,1152]{2,1,0:T(8,128)S(1)}, f32[2,48,1152]{2,1,0:T(8,128)S(1)}, u32[]{:S(2)}, u32[]{:S(2)}) %collective-permute-start.16) | collective-permute-done | bytes 442400 | tf_op jit(solution)/shard_map/ppermute | solution.py:97
  572.6 22.6 %collective-permute-done.13 = f32[1,48,1152]{2,1,0:T(8,128)S(1)} collective-permute-done((f32[1,48,1152]{2,1,0:T(8,128)S(1)}, f32[1,48,1152]{2,1,0:T(8,128)S(1)}, u32[]{:S(2)}, u32[]{:S(2)}) %collective-permute-start.13) | collective-permute-done | bytes 221216 | tf_op jit(solution)/shard_map/ppermute | solution.py:97
  603.1 19.3 %collective-permute-done.37 = f32[1,48,1536]{2,1,0:T(8,128)S(1)} collective-permute-done((f32[1,48,1536]{2,1,0:T(8,128)S(1)}, f32[1,48,1536]{2,1,0:T(8,128)S(1)}, u32[]{:S(2)}, u32[]{:S(2)}) %collective-permute-start.37) | collective-permute-done | bytes 294944 | tf_op jit(solution)/shard_map/ppermute | solution.py:97
  622.5 5.1 collective-permute-done.41
  (645 shorter events, 261.3 us)
Async XLA Ops:
  23.4 19.1 %collective-permute-start.1 = (f32[1,256,768]{2,1,0:T(8,128)S(1)}, f32[1,256,768]{2,1,0:T(8,128)S(1)}, u32[]{:S(2)}, u32[]{:S(2)}) collective-permute-start(f32[1,256,768]{2,1,0:T(8,128)S(1)} %convolution_bitcast_fusion.3), channel_id=1, source_target_pairs={{0,1},{1,0},{2,3},{3,2},{4,5},{5,4},{6,7},{7,6},{8,9},{9,8},{10,11... | collective-permute-start | bytes 2359304 | tf_op jit(solution)/shard_map/ppermute | solution.py:41
  54.4 18.3 %collective-permute-start.2 = (f32[1,256,768]{2,1,0:T(8,128)S(1)}, f32[1,256,768]{2,1,0:T(8,128)}, u32[]{:S(2)}, u32[]{:S(2)}) collective-permute-start(f32[1,256,768]{2,1,0:T(8,128)S(1)} %fusion.77), channel_id=1, source_target_pairs={{0,1},{1,0},{2,3},{3,2},{4,5},{5,4},{6,7},{7,6},{8,9},{9,8},{10,11... | collective-permute-start | bytes 2359304 | tf_op jit(solution)/shard_map/ppermute | solution.py:41
  89.0 17.2 %collective-permute-start.3 = (f32[1,256,768]{2,1,0:T(8,128)S(1)}, f32[1,256,768]{2,1,0:T(8,128)S(1)}, u32[]{:S(2)}, u32[]{:S(2)}) collective-permute-start(f32[1,256,768]{2,1,0:T(8,128)S(1)} %convolution_bitcast_fusion.2), channel_id=1, source_target_pairs={{0,1},{1,0},{2,3},{3,2},{4,5},{5,4},{6,7},{7,6},{8,9},{9,8},{10,11... | collective-permute-start | bytes 2359304 | tf_op jit(solution)/shard_map/ppermute | solution.py:41
  121.3 20.5 %collective-permute-start.5 = (f32[1,256,768]{2,1,0:T(8,128)S(1)}, f32[1,256,768]{2,1,0:T(8,128)S(1)}, u32[]{:S(2)}, u32[]{:S(2)}) collective-permute-start(f32[1,256,768]{2,1,0:T(8,128)S(1)} %fusion.80), channel_id=1, source_target_pairs={{0,1},{1,0},{2,3},{3,2},{4,5},{5,4},{6,7},{7,6},{8,9},{9,8},{10,11... | collective-permute-start | bytes 2359304 | tf_op jit(solution)/shard_map/ppermute | solution.py:41
  126.6 27.8 %collective-permute-start.4 = (f32[1,256,768]{2,1,0:T(8,128)S(1)}, f32[1,256,768]{2,1,0:T(8,128)S(1)}, u32[]{:S(2)}, u32[]{:S(2)}) collective-permute-start(f32[1,256,768]{2,1,0:T(8,128)S(1)} %fusion.83), channel_id=1, source_target_pairs={{0,1},{1,0},{2,3},{3,2},{4,5},{5,4},{6,7},{7,6},{8,9},{9,8},{10,11... | collective-permute-start | bytes 2359304 | tf_op jit(solution)/shard_map/ppermute | solution.py:41
  174.3 31.3 %collective-permute-start.6 = (f32[1,256,768]{2,1,0:T(8,128)}, f32[1,256,768]{2,1,0:T(8,128)}, u32[]{:S(2)}, u32[]{:S(2)}) collective-permute-start(f32[1,256,768]{2,1,0:T(8,128)} %fusion.71), channel_id=1, source_target_pairs={{0,1},{1,0},{2,3},{3,2},{4,5},{5,4},{6,7},{7,6},{8,9},{9,8},{10,11... | collective-permute-start | bytes 2359304 | tf_op jit(solution)/shard_map/ppermute | solution.py:41
  215.5 16.0 %collective-permute-start.22 = (f32[1,6528]{1,0:T(1,128)}, f32[1,6528]{1,0:T(1,128)}, u32[]{:S(2)}, u32[]{:S(2)}) collective-permute-start(f32[1,6528]{1,0:T(1,128)} %pad_maximum_fusion.14), channel_id=1, source_target_pairs={{0,30},{2,0},{4,2},{6,4},{8,6},{10,8},{12,10},{14,12},{16,14},{18,... | collective-permute-start | bytes 78344 | tf_op jit(solution)/shard_map/ppermute | solution.py:16
  227.4 31.9 %collective-permute-start.7 = (f32[1,256,768]{2,1,0:T(8,128)}, f32[1,256,768]{2,1,0:T(8,128)}, u32[]{:S(2)}, u32[]{:S(2)}) collective-permute-start(f32[1,256,768]{2,1,0:T(8,128)} %fusion.74), channel_id=1, source_target_pairs={{0,1},{1,0},{2,3},{3,2},{4,5},{5,4},{6,7},{7,6},{8,9},{9,8},{10,11... | collective-permute-start | bytes 2359304 | tf_op jit(solution)/shard_map/ppermute | solution.py:41
  240.5 159.1 %collective-permute-start.42 = (f32[384,1536]{1,0:T(8,128)}, f32[384,1536]{1,0:T(8,128)}, u32[]{:S(2)}, u32[]{:S(2)}) collective-permute-start(f32[384,1536]{1,0:T(8,128)} %fusion.188), channel_id=1, source_target_pairs={{0,2},{2,0},{4,6},{6,4},{8,10},{10,8},{12,14},{14,12},{16,18},{18,... | collective-permute-start | bytes 7077896 | tf_op jit(solution)/shard_map/ppermute | solution.py:87
  248.2 155.3 %collective-permute-start.46 = (f32[384,1536]{1,0:T(8,128)}, f32[384,1536]{1,0:T(8,128)}, u32[]{:S(2)}, u32[]{:S(2)}) collective-permute-start(f32[384,1536]{1,0:T(8,128)} %fusion.189), channel_id=1, source_target_pairs={{0,2},{2,0},{4,6},{6,4},{8,10},{10,8},{12,14},{14,12},{16,18},{18,... | collective-permute-start | bytes 7077896 | tf_op jit(solution)/shard_map/ppermute | solution.py:87
  280.3 18.8 %collective-permute-start.8 = (f32[1,256,768]{2,1,0:T(8,128)}, f32[1,256,768]{2,1,0:T(8,128)}, u32[]{:S(2)}, u32[]{:S(2)}) collective-permute-start(f32[1,256,768]{2,1,0:T(8,128)} %fusion.68), channel_id=1, source_target_pairs={{0,1},{1,0},{2,3},{3,2},{4,5},{5,4},{6,7},{7,6},{8,9},{9,8},{10,11... | collective-permute-start | bytes 2359304 | tf_op jit(solution)/shard_map/ppermute | solution.py:41
  292.0 116.3 %collective-permute-start.34 = (f32[384,1536]{1,0:T(8,128)}, f32[384,1536]{1,0:T(8,128)}, u32[]{:S(2)}, u32[]{:S(2)}) collective-permute-start(f32[384,1536]{1,0:T(8,128)} %fusion.220), channel_id=1, source_target_pairs={{0,2},{2,0},{4,6},{6,4},{8,10},{10,8},{12,14},{14,12},{16,18},{18,... | collective-permute-start | bytes 7077896 | tf_op jit(solution)/shard_map/ppermute | solution.py:87
  292.6 120.1 %collective-permute-start.38 = (f32[384,1536]{1,0:T(8,128)}, f32[384,1536]{1,0:T(8,128)}, u32[]{:S(2)}, u32[]{:S(2)}) collective-permute-start(f32[384,1536]{1,0:T(8,128)} %fusion.221), channel_id=1, source_target_pairs={{0,2},{2,0},{4,6},{6,4},{8,10},{10,8},{12,14},{14,12},{16,18},{18,... | collective-permute-start | bytes 7077896 | tf_op jit(solution)/shard_map/ppermute | solution.py:87
  304.2 18.2 %collective-permute-start.18 = (f32[1,6528]{1,0:T(1,128)S(1)}, f32[1,6528]{1,0:T(1,128)S(1)}, u32[]{:S(2)}, u32[]{:S(2)}) collective-permute-start(f32[1,6528]{1,0:T(1,128)S(1)} %pad_maximum_fusion.13), channel_id=1, source_target_pairs={{0,30},{2,0},{4,2},{6,4},{8,6},{10,8},{12,10},{14,12},{16,14},{18,... | collective-permute-start | bytes 78344 | tf_op jit(solution)/shard_map/ppermute | solution.py:16
  382.7 34.3 %collective-permute-start.10 = (f32[384,1152]{1,0:T(8,128)}, f32[384,1152]{1,0:T(8,128)}, u32[]{:S(2)}, u32[]{:S(2)}) collective-permute-start(f32[384,1152]{1,0:T(8,128)} %fusion.216), channel_id=1, source_target_pairs={{0,2},{2,0},{4,6},{6,4},{8,10},{10,8},{12,14},{14,12},{16,18},{18,... | collective-permute-start | bytes 5308424 | tf_op jit(solution)/shard_map/ppermute | solution.py:87
  399.6 21.3 %collective-permute-start.14 = (f32[384,1152]{1,0:T(8,128)}, f32[384,1152]{1,0:T(8,128)S(1)}, u32[]{:S(2)}, u32[]{:S(2)}) collective-permute-start(f32[384,1152]{1,0:T(8,128)} %fusion.217), channel_id=1, source_target_pairs={{0,2},{2,0},{4,6},{6,4},{8,10},{10,8},{12,14},{14,12},{16,18},{18,... | collective-permute-start | bytes 5308424 | tf_op jit(solution)/shard_map/ppermute | solution.py:87
  403.4 28.9 %collective-permute-start.43 = (f32[4,48,1536]{2,1,0:T(8,128)S(1)}, f32[4,48,1536]{2,1,0:T(8,128)S(1)}, u32[]{:S(2)}, u32[]{:S(2)}) collective-permute-start(f32[4,48,1536]{2,1,0:T(8,128)S(1)} %dynamic-slice_bitcast_fusion.1), channel_id=1, source_target_pairs={{0,4},{2,6},{4,0},{6,2},{8,12},{10,14},{12,8},{14,10},{16,20},{18,... | collective-permute-start | bytes 3538952 | tf_op jit(solution)/shard_map/ppermute | solution.py:97
  408.3 49.3 %collective-permute-start.47 = (f32[4,48,1536]{2,1,0:T(8,128)S(1)}, f32[4,48,1536]{2,1,0:T(8,128)S(1)}, u32[]{:S(2)}, u32[]{:S(2)}) collective-permute-start(f32[4,48,1536]{2,1,0:T(8,128)S(1)} %dynamic-slice_bitcast_fusion), channel_id=1, source_target_pairs={{0,4},{2,6},{4,0},{6,2},{8,12},{10,14},{12,8},{14,10},{16,20},{18,... | collective-permute-start | bytes 3538952 | tf_op jit(solution)/shard_map/ppermute | solution.py:97
  412.7 132.6 %collective-permute-start.35 = (f32[4,48,1536]{2,1,0:T(8,128)S(1)}, f32[4,48,1536]{2,1,0:T(8,128)S(1)}, u32[]{:S(2)}, u32[]{:S(2)}) collective-permute-start(f32[4,48,1536]{2,1,0:T(8,128)S(1)} %dynamic-slice_bitcast_fusion.3), channel_id=1, source_target_pairs={{0,4},{2,6},{4,0},{6,2},{8,12},{10,14},{12,8},{14,10},{16,20},{18,... | collective-permute-start | bytes 3538952 | tf_op jit(solution)/shard_map/ppermute | solution.py:97
  417.1 130.6 %collective-permute-start.39 = (f32[4,48,1536]{2,1,0:T(8,128)S(1)}, f32[4,48,1536]{2,1,0:T(8,128)S(1)}, u32[]{:S(2)}, u32[]{:S(2)}) collective-permute-start(f32[4,48,1536]{2,1,0:T(8,128)S(1)} %dynamic-slice_bitcast_fusion.2), channel_id=1, source_target_pairs={{0,4},{2,6},{4,0},{6,2},{8,12},{10,14},{12,8},{14,10},{16,20},{18,... | collective-permute-start | bytes 3538952 | tf_op jit(solution)/shard_map/ppermute | solution.py:97
  421.0 106.2 %collective-permute-start.11 = (f32[4,48,1152]{2,1,0:T(8,128)S(1)}, f32[4,48,1152]{2,1,0:T(8,128)S(1)}, u32[]{:S(2)}, u32[]{:S(2)}) collective-permute-start(f32[4,48,1152]{2,1,0:T(8,128)S(1)} %dynamic-slice_bitcast_fusion.5), channel_id=1, source_target_pairs={{0,4},{2,6},{4,0},{6,2},{8,12},{10,14},{12,8},{14,10},{16,20},{18,... | collective-permute-start | bytes 2654216 | tf_op jit(solution)/shard_map/ppermute | solution.py:97
  432.3 112.8 %collective-permute-start.15 = (f32[4,48,1152]{2,1,0:T(8,128)S(1)}, f32[4,48,1152]{2,1,0:T(8,128)S(1)}, u32[]{:S(2)}, u32[]{:S(2)}) collective-permute-start(f32[4,48,1152]{2,1,0:T(8,128)S(1)} %dynamic-slice_bitcast_fusion.4), channel_id=1, source_target_pairs={{0,4},{2,6},{4,0},{6,2},{8,12},{10,14},{12,8},{14,10},{16,20},{18,... | collective-permute-start | bytes 2654216 | tf_op jit(solution)/shard_map/ppermute | solution.py:97
  457.6 13.5 %collective-permute-start.44 = (f32[2,48,1536]{2,1,0:T(8,128)S(1)}, f32[2,48,1536]{2,1,0:T(8,128)S(1)}, u32[]{:S(2)}, u32[]{:S(2)}) collective-permute-start(f32[2,48,1536]{2,1,0:T(8,128)S(1)} %dynamic-slice_bitcast_fusion.7), channel_id=1, source_target_pairs={{0,8},{2,10},{4,12},{6,14},{8,0},{10,2},{12,4},{14,6},{16,24},{18,... | collective-permute-start | bytes 1769480 | tf_op jit(solution)/shard_map/ppermute | solution.py:97
  483.7 64.2 %collective-permute-start.45 = (f32[1,48,1536]{2,1,0:T(8,128)S(1)}, f32[1,48,1536]{2,1,0:T(8,128)S(1)}, u32[]{:S(2)}, u32[]{:S(2)}) collective-permute-start(f32[1,48,1536]{2,1,0:T(8,128)S(1)} %constant_dynamic-slice_fusion.4), channel_id=1, source_target_pairs={{0,16},{2,18},{4,20},{6,22},{8,24},{10,26},{12,28},{14,30},{16,0},... | collective-permute-start | bytes 884744 | tf_op jit(solution)/shard_map/ppermute | solution.py:97
  527.1 22.9 %collective-permute-start.49 = (f32[1,48,1536]{2,1,0:T(8,128)S(1)}, f32[1,48,1536]{2,1,0:T(8,128)S(1)}, u32[]{:S(2)}, u32[]{:S(2)}) collective-permute-start(f32[1,48,1536]{2,1,0:T(8,128)S(1)} %constant_dynamic-slice_fusion.1), channel_id=1, source_target_pairs={{0,16},{2,18},{4,20},{6,22},{8,24},{10,26},{12,28},{14,30},{16,0},... | collective-permute-start | bytes 884744 | tf_op jit(solution)/shard_map/ppermute | solution.py:97
  545.3 27.2 %collective-permute-start.16 = (f32[2,48,1152]{2,1,0:T(8,128)S(1)}, f32[2,48,1152]{2,1,0:T(8,128)S(1)}, u32[]{:S(2)}, u32[]{:S(2)}) collective-permute-start(f32[2,48,1152]{2,1,0:T(8,128)S(1)} %dynamic-slice_bitcast_fusion.10), channel_id=1, source_target_pairs={{0,8},{2,10},{4,12},{6,14},{8,0},{10,2},{12,4},{14,6},{16,24},{18,... | collective-permute-start | bytes 1327112 | tf_op jit(solution)/shard_map/ppermute | solution.py:97
  547.6 51.7 %collective-permute-start.36 = (f32[2,48,1536]{2,1,0:T(8,128)S(1)}, f32[2,48,1536]{2,1,0:T(8,128)S(1)}, u32[]{:S(2)}, u32[]{:S(2)}) collective-permute-start(f32[2,48,1536]{2,1,0:T(8,128)S(1)} %dynamic-slice_bitcast_fusion.9), channel_id=1, source_target_pairs={{0,8},{2,10},{4,12},{6,14},{8,0},{10,2},{12,4},{14,6},{16,24},{18,... | collective-permute-start | bytes 1769480 | tf_op jit(solution)/shard_map/ppermute | solution.py:97
  547.9 55.0 %collective-permute-start.40 = (f32[2,48,1536]{2,1,0:T(8,128)S(1)}, f32[2,48,1536]{2,1,0:T(8,128)S(1)}, u32[]{:S(2)}, u32[]{:S(2)}) collective-permute-start(f32[2,48,1536]{2,1,0:T(8,128)S(1)} %dynamic-slice_bitcast_fusion.8), channel_id=1, source_target_pairs={{0,8},{2,10},{4,12},{6,14},{8,0},{10,2},{12,4},{14,6},{16,24},{18,... | collective-permute-start | bytes 1769480 | tf_op jit(solution)/shard_map/ppermute | solution.py:97
  558.3 36.9 %collective-permute-start.13 = (f32[1,48,1152]{2,1,0:T(8,128)S(1)}, f32[1,48,1152]{2,1,0:T(8,128)S(1)}, u32[]{:S(2)}, u32[]{:S(2)}) collective-permute-start(f32[1,48,1152]{2,1,0:T(8,128)S(1)} %constant_dynamic-slice_fusion.22), channel_id=1, source_target_pairs={{0,16},{2,18},{4,20},{6,22},{8,24},{10,26},{12,28},{14,30},{16,0},... | collective-permute-start | bytes 663560 | tf_op jit(solution)/shard_map/ppermute | solution.py:97
  572.6 25.9 %collective-permute-start.17 = (f32[1,48,1152]{2,1,0:T(8,128)S(1)}, f32[1,48,1152]{2,1,0:T(8,128)S(1)}, u32[]{:S(2)}, u32[]{:S(2)}) collective-permute-start(f32[1,48,1152]{2,1,0:T(8,128)S(1)} %constant_dynamic-slice_fusion.19), channel_id=1, source_target_pairs={{0,16},{2,18},{4,20},{6,22},{8,24},{10,26},{12,28},{14,30},{16,0},... | collective-permute-start | bytes 663560 | tf_op jit(solution)/shard_map/ppermute | solution.py:97
  599.4 23.0 %collective-permute-start.37 = (f32[1,48,1536]{2,1,0:T(8,128)S(1)}, f32[1,48,1536]{2,1,0:T(8,128)S(1)}, u32[]{:S(2)}, u32[]{:S(2)}) collective-permute-start(f32[1,48,1536]{2,1,0:T(8,128)S(1)} %constant_dynamic-slice_fusion.10), channel_id=1, source_target_pairs={{0,16},{2,18},{4,20},{6,22},{8,24},{10,26},{12,28},{14,30},{16,0},... | collective-permute-start | bytes 884744 | tf_op jit(solution)/shard_map/ppermute | solution.py:97
  603.0 24.5 %collective-permute-start.41 = (f32[1,48,1536]{2,1,0:T(8,128)S(1)}, f32[1,48,1536]{2,1,0:T(8,128)S(1)}, u32[]{:S(2)}, u32[]{:S(2)}) collective-permute-start(f32[1,48,1536]{2,1,0:T(8,128)S(1)} %constant_dynamic-slice_fusion.7), channel_id=1, source_target_pairs={{0,16},{2,18},{4,20},{6,22},{8,24},{10,26},{12,28},{14,30},{16,0},... | collective-permute-start | bytes 884744 | tf_op jit(solution)/shard_map/ppermute | solution.py:97
  (178 other events, 1185.3 us)
